TPU v7x, 32 devices: a whole 2x2x4 slice. The times are simulated.
32 devices in a mesh: groups: 2 (over y), row: 4 (over z), col: 4 (over x, core).
Axes of the slice: x: 2, y: 2, z: 4, core: 2. Of those that a mesh axis runs over, the one named last changes fastest.
Arguments:
- alignment: bfloat16 [256, 128, 256], P(('groups', 'row'), 'col'), parts along dimension 0, may hold values from -6 to 6
- sequence_mask: int32 [256], P('groups'), parts along dimension 0, may hold values 0 or 1
- residue_mask: int32 [256], P('groups'), parts along dimension 0, may hold values 0 or 1
- layer_norm_gain: float32 [256], replicated, may hold values from 0.5 to 1.5
- norm_shift: float32 [256], replicated, may hold values from -3 to 3
- proj_weight: bfloat16 [256, 64], replicated, may hold values from -0.375 to 0.375
- proj_bias: float32 [64], replicated, may hold values from -3 to 3
- out_weight: bfloat16 [1024, 128], replicated, may hold values from -2 to 2
- out_bias: float32 [128], replicated, may hold values from -4 to 4
- cotangent: bfloat16 [256, 128, 128], P(('groups', 'row'), 'col'), parts along dimension 0, may hold values from -2 to 2
Outputs:
- pair_output_update: bfloat16 [256, 128, 128], P(('groups', 'row'), 'col'), parts along dimension 0
- alignment_gradient: bfloat16 [256, 128, 256], P(('groups', 'row'), 'col'), parts along dimension 0
- norm_gain_gradient: float32 [512], P('groups'), parts along dimension 0
- norm_shift_gradient: float32 [512], P('groups'), parts along dimension 0
- projection_weight_gradient: float32 [512, 64], P('groups'), parts along dimension 0
- projection_bias_gradient: float32 [128], P('groups'), parts along dimension 0
- output_weight_gradient: float32 [2048, 128], P('groups'), parts along dimension 0
There are 2 independent parts, one for each index of `groups`. A program takes and returns all parts, laid end to end along the dimension named above; an argument that names none is the same for every part. Nothing has to cross between parts.
All inputs are finite; a program needn't handle non-finite values.
Results may differ from a plain program's by a relative error of at most 0.0074.
Values may be sent and summed in bfloat16 or wider, within the bound.
A program may use at most 64 MiB of HBM per device.

v0:
```python
import jax
import jax.numpy as jnp
from jax import lax
from jax.sharding import PartitionSpec as P

EPSILON = 1e-05


def normalize(values, layer_norm_gain, norm_shift):
    widened = values.astype(jnp.float32)
    centred = widened - jnp.mean(widened, axis=-1, keepdims=True)
    inverse_deviation = lax.rsqrt(jnp.mean(centred * centred, axis=-1, keepdims=True) + EPSILON)
    scaled_product = centred * inverse_deviation
    return (
        scaled_product,
        inverse_deviation,
        (scaled_product * layer_norm_gain + norm_shift).astype(jnp.bfloat16),
    )


def layer_norm_backward_pass(
    normalized_input_gradient, scaled_product, inverse_deviation, layer_norm_gain
):
    grad_scaled = normalized_input_gradient * layer_norm_gain
    first = jnp.mean(grad_scaled, axis=-1, keepdims=True)
    second = jnp.mean(grad_scaled * scaled_product, axis=-1, keepdims=True)
    return inverse_deviation * (grad_scaled - first - scaled_product * second)


def outer_block(left_block, right_flat, hidden, width_j):
    product = lax.dot_general(
        left_block, right_flat, (((0,), (0,)), ((), ())), preferred_element_type=jnp.float32
    )
    count_i = left_block.shape[1] // hidden
    product = product.reshape(count_i, hidden, width_j, hidden).transpose(0, 2, 1, 3)
    return product.reshape(count_i * width_j, hidden * hidden).astype(jnp.bfloat16)


def outer_adjoint(grad_outer, count_i, width_j, hidden):
    arranged = grad_outer.reshape(count_i, width_j, hidden, hidden).transpose(0, 2, 1, 3)
    return arranged.reshape(count_i * hidden, width_j * hidden)


def shards(
    alignment,
    sequence_mask,
    residue_mask,
    layer_norm_gain,
    norm_shift,
    proj_weight,
    proj_bias,
    out_weight,
    out_bias,
    cotangent,
):
    row_count = lax.axis_size("row")
    col_count = lax.axis_size("col")
    factor = col_count // row_count
    row_index = lax.axis_index("row")
    col_index = lax.axis_index("col")
    seq_local, res_local, channels = alignment.shape
    hidden = proj_weight.shape[1] // 2
    pair_width = out_weight.shape[1]
    tile_rows = res_local * factor
    scaled_product, inverse_deviation, normed = normalize(alignment, layer_norm_gain, norm_shift)
    seq_here = lax.dynamic_slice_in_dim(sequence_mask, row_index * seq_local, seq_local)
    res_here = lax.dynamic_slice_in_dim(residue_mask, col_index * res_local, res_local)
    live = (seq_here[:, None] * res_here[None, :]).astype(jnp.float32)
    projected = jnp.dot(
        normed.reshape(-1, channels), proj_weight, preferred_element_type=jnp.float32
    )
    projected = projected.reshape(seq_local, res_local, 2 * hidden) + proj_bias
    masked = (projected * live[:, :, None]).astype(jnp.bfloat16)
    stacked = jnp.stack(
        [
            masked[:, :, :hidden].reshape(seq_local, res_local * hidden),
            masked[:, :, hidden:].reshape(seq_local, res_local * hidden),
        ],
        axis=1,
    )
    gathered = lax.all_gather(stacked, "row", axis=0, tiled=True)
    left_column = gathered[:, 0]
    right_flat = gathered[:, 1]
    everything = lax.all_gather(left_column, "col", axis=1, tiled=True)
    left_flat = lax.dynamic_slice_in_dim(
        everything, row_index * tile_rows * hidden, tile_rows * hidden, 1
    )
    kept_count = jnp.sum(sequence_mask).astype(jnp.float32)
    tile_live = lax.dynamic_slice_in_dim(residue_mask, row_index * tile_rows, tile_rows).astype(
        jnp.float32
    )
    column_live = res_here.astype(jnp.float32)
    block_rows = min(tile_rows, max(1, 1024 // res_local))
    all_seqs = left_flat.shape[0]

    def advance(running, block_index):
        grad_out_w, grad_right = running
        offset = block_index * block_rows
        left_block = lax.dynamic_slice_in_dim(left_flat, offset * hidden, block_rows * hidden, 1)
        products = outer_block(left_block, right_flat, hidden, res_local)
        preact = jnp.dot(products, out_weight, preferred_element_type=jnp.float32) + out_bias
        live_rows = lax.dynamic_slice_in_dim(tile_live, offset, block_rows)
        divisor = jnp.maximum(kept_count * live_rows[:, None] * column_live[None, :], 1.0).reshape(
            -1, 1
        )
        pair_block = (preact / divisor).astype(jnp.bfloat16)
        cot_block = (
            lax.dynamic_slice_in_dim(cotangent, offset, block_rows, 0)
            .reshape(-1, pair_width)
            .astype(jnp.float32)
        )
        grad_pre = (cot_block / divisor).astype(jnp.bfloat16)
        grad_out_w = grad_out_w + lax.dot_general(
            products, grad_pre, (((0,), (0,)), ((), ())), preferred_element_type=jnp.float32
        )
        grad_outer = jnp.dot(grad_pre, out_weight.T, preferred_element_type=jnp.float32).astype(
            jnp.bfloat16
        )
        grad_pairs = outer_adjoint(grad_outer, block_rows, res_local, hidden)
        grad_left = lax.dot_general(
            right_flat, grad_pairs, (((1,), (1,)), ((), ())), preferred_element_type=jnp.float32
        )
        grad_right = grad_right + jnp.dot(
            left_block, grad_pairs, preferred_element_type=jnp.float32
        )
        return ((grad_out_w, grad_right), (pair_block, grad_left))

    initial = (
        jnp.zeros((hidden * hidden, pair_width), jnp.float32),
        jnp.zeros((all_seqs, res_local * hidden), jnp.float32),
    )
    (grad_out_w, grad_right), (pair_blocks, grad_lefts) = lax.scan(
        advance, initial, jnp.arange(tile_rows // block_rows, dtype=jnp.int32)
    )
    pair_output_update = pair_blocks.reshape(tile_rows, res_local, pair_width)
    left_tile = grad_lefts.transpose(1, 0, 2).reshape(all_seqs, tile_rows * hidden)
    regrouped = lax.all_to_all(left_tile, "row", split_axis=0, concat_axis=1, tiled=True)
    grad_left = lax.psum_scatter(regrouped, "col", scatter_dimension=1, tiled=True)
    grad_right = lax.psum_scatter(grad_right, "row", scatter_dimension=0, tiled=True)
    grad_projected = (
        jnp.concatenate(
            [
                grad_left.reshape(seq_local, res_local, hidden),
                grad_right.reshape(seq_local, res_local, hidden),
            ],
            axis=-1,
        )
        * live[:, :, None]
    )
    grad_low = grad_projected.astype(jnp.bfloat16)
    normalized_input_gradient = jnp.dot(
        grad_low.reshape(-1, 2 * hidden), proj_weight.T, preferred_element_type=jnp.float32
    ).reshape(seq_local, res_local, channels)
    weight_local = lax.dot_general(
        normed.reshape(-1, channels),
        grad_low.reshape(-1, 2 * hidden),
        (((0,), (0,)), ((), ())),
        preferred_element_type=jnp.float32,
    )
    bias_local = jnp.sum(grad_projected, axis=(0, 1))
    gain_local = jnp.sum(normalized_input_gradient * scaled_product, axis=(0, 1))
    shift_local = jnp.sum(normalized_input_gradient, axis=(0, 1))
    alignment_gradient = layer_norm_backward_pass(
        normalized_input_gradient, scaled_product, inverse_deviation, layer_norm_gain
    ).astype(jnp.bfloat16)
    summed_products = lax.psum(
        (grad_out_w, weight_local, bias_local, gain_local, shift_local), ("row", "col")
    )
    return (
        pair_output_update,
        alignment_gradient,
        summed_products[3],
        summed_products[4],
        summed_products[1],
        summed_products[2],
        summed_products[0],
    )


def solution(mesh):
    return jax.shard_map(
        shards,
        mesh=mesh,
        in_specs=(
            P(("groups", "row"), "col", None),
            P("groups"),
            P("groups"),
            P(),
            P(),
            P(),
            P(),
            P(),
            P(),
            P(("groups", "row"), "col", None),
        ),
        out_specs=(
            P(("groups", "row"), "col", None),
            P(("groups", "row"), "col", None),
            P("groups"),
            P("groups"),
            P("groups", None),
            P("groups"),
            P("groups", None),
        ),
        check_vma=False,
    )
```

profile of v0, /device:TPU:0, one launch (start us, length us, event | category | flops | bytes accessed | tf_op | source)
XLA Modules:
  0.0 232.5 jit_solution(14596314626865325024)
XLA Ops:
  7.2 1.3 convert_reduce_fusion
  8.5 1.4 fusion.17
  11.5 1.6 fusion.8
  13.8 17.4 %all_gather.6 = bf16[128,2,1024]{2,0,1:T(8,128)(2,1)S(1)} all-gather(bf16[32,2,1024]{2,0,1:T(8,128)(2,1)S(1)} %pad_maximum_fusion), channel_id=1, replica_groups=mesh['groups'=2,'row'=4,'col'=4] {'row'}, dimensions={0}, use_global_device_ids=true | all-gather | bytes 655360 | tf_op jit(solution)/shard_map/all_gather | solution.py:81
  34.6 8.0 %reshape.151 = bf16[32,32,32,32]{3,2,1,0:T(8,128)(2,1)} reshape(bf16[1024,1024]{1,0:T(8,128)(2,1)S(1)} %convolution_convert_fusion) | data formatting | bytes 4194304 | tf_op jit(solution)/shard_map/while/body/eval_jaxpr/reshape | solution.py:40
  42.6 10.5 %copy.21 = bf16[32,32,32,32]{3,2,1,0:T(8,128)(2,1)} copy(bf16[32,32,32,32]{3,1,2,0:T(8,128)(2,1)} %bitcast.59) | data formatting | bytes 4194304 | tf_op jit(solution)/shard_map/while/body/eval_jaxpr/transpose | solution.py:40
  53.1 11.3 %reshape.159 = bf16[1024,1024,1]{1,0,2:T(8,128)(2,1)S(1)} reshape(bf16[32,32,32,32]{3,2,1,0:T(8,128)(2,1)} %copy.21) | data formatting | bytes 4194304 | tf_op jit(solution)/shard_map/while/body/eval_jaxpr/reshape | solution.py:41
  65.3 16.4 %all_to_all.16 = f32[4,32,1024]{2,1,0:T(8,128)S(1)} all-to-all(f32[4,32,1024]{2,1,0:T(8,128)S(1)} %fusion.34), channel_id=1, replica_groups=mesh['groups'=2,'row'=4,'col'=4] {'row'}, dimensions={0} | all-to-all | bytes 1048576 | tf_op jit(solution)/shard_map/all_to_all | solution.py:137
  82.7 11.4 %reshape.152 = bf16[1024,1024]{1,0:T(8,128)(2,1)S(1)} reshape(bf16[32,32,32,32]{3,2,1,0:T(8,128)(2,1)} %copy.21) | data formatting | bytes 4194304 | tf_op jit(solution)/shard_map/while/body/eval_jaxpr/reshape | solution.py:41
  94.5 2.2 fusion.19
  96.8 1.0 dynamic-slice_bitcast_fusion
  98.0 5.6 %convert_bitcast_fusion = bf16[32,32,32,32]{3,2,1,0:T(8,128)(2,1)} fusion(bf16[32,32,128,1]{2,1,3,0:T(8,128)(2,1)S(1)} %bitcast.64, bf16[32,32,128,1]{2,1,0,3:T(8,128)(2,1)S(1)} %bitcast.63), kind=kOutput, calls=%fused_computation | convolution fusion | flops 269484032 | bytes 2621440 | tf_op jit(solution)/shard_map/while/body/eval_jaxpr/dot_general | solution.py:31
  103.6 11.3 %convert_element_type.78 = bf16[1024,1024]{1,0:T(8,128)(2,1)S(1)} reshape(bf16[32,32,32,32]{3,2,1,0:T(8,128)(2,1)} %convert_bitcast_fusion) | data formatting | bytes 4194304 | tf_op jit(solution)/shard_map/while/body/eval_jaxpr/convert_element_type | solution.py:36
  114.9 1.4 fusion.9
  116.4 1.5 fusion.35
  117.9 1.1 concatenate.9
  119.1 9.1 %reduce-scatter.5.cloned.1.call-done = f32[32,1024]{1,0:T(8,128)} async-done(((f32[128,1024]{1,0:T(8,128)}), f32[32,1024]{1,0:T(8,128)}) %reduce-scatter.5.cloned.1.call-update) | async-done | bytes 131088 | tf_op jit(solution)/shard_map/reduce_scatter | solution.py:139
  128.2 1.1 concatenate.10
  129.6 1.2 convolution_bitcast_fusion
  131.6 30.2 %all-reduce = (f32[256]{0:T(256)}, f32[256]{0:T(256)}, f32[64]{0:T(128)}) all-reduce(f32[256]{0:T(256)S(1)} %get-tuple-element.33, f32[256]{0:T(256)S(1)} %get-tuple-element.36, f32[64]{0:T(128)S(1)} %get-tuple-element.55), channel_id=1, replica_groups=mesh['groups'=2,'row'=4,'col'=4] {'row','col'}, use_global_device_ids=true, to_apply=%region_8.9 | all-reduce | flops 576 | bytes 4608 | tf_op jit(solution)/shard_map/psum | solution.py:166
  161.8 1.4 fusion.15
  163.2 59.4 %all-reduce.4.cloned.1.call-done = (f32[256,64]{0,1:T(8,128)}, f32[1024,128]{1,0:T(8,128)}) async-done(((f32[256,64]{0,1:T(8,128)}, f32[1024,128]{1,0:T(8,128)}), (f32[256,64]{0,1:T(8,128)}, f32[1024,128]{1,0:T(8,128)})) %all-reduce.4.cloned.1.call-update) | async-done | bytes 589840 | tf_op jit(solution)/shard_map/psum | solution.py:166
  222.7 1.5 copy.27
  224.1 1.9 copy.28
  (52 shorter events, 8.6 us)
Async XLA Ops:
  7.2 26.7 %copy-start = (bf16[1024,128]{1,0:T(8,128)(2,1)S(1)}, bf16[1024,128]{1,0:T(8,128)(2,1)}, u32[]{:S(2)}) copy-start(bf16[1024,128]{1,0:T(8,128)(2,1)} %param.17) | copy-start | bytes 786436
  7.2 87.4 %all-gather.3.cloned.1.call-start = ((), (), s32[]{:S(2)}) async-start(), calls=%async_computation.5 | async-start | bytes 1310720 | tf_op jit(solution)/shard_map/all_gather | solution.py:84
  13.1 19.0 %copy-start.7 = (s32[128]{0:T(128)S(1)}, s32[128]{0:T(128)}, u32[]{:S(2)}) copy-start(s32[128]{0:T(128)} %param.11) | copy-start | bytes 1540
  13.1 20.3 %copy-start.3 = (s32[128]{0:T(128)S(1)}, s32[128]{0:T(128)}, u32[]{:S(2)}) copy-start(s32[128]{0:T(128)} %param.12) | copy-start | bytes 1540
  13.1 20.5 %copy-start.2 = (bf16[32,32,128]{2,1,0:T(8,128)(2,1)S(1)}, bf16[32,32,128]{2,1,0:T(8,128)(2,1)}, u32[]{:S(2)}) copy-start(bf16[32,32,128]{2,1,0:T(8,128)(2,1)} %param.19) | copy-start | bytes 786436
  32.0 85.9 %reduce-scatter.3.cloned.1.call-start = ((), (), s32[]{:S(2)}) async-start(), calls=%async_computation.3 | async-start | bytes 655360 | tf_op jit(solution)/shard_map/reduce_scatter | solution.py:138
  82.5 45.7 %reduce-scatter.5.cloned.1.call-start = ((), (), s32[]{:S(2)}) async-start(), calls=%async_computation.4 | async-start | bytes 655360 | tf_op jit(solution)/shard_map/reduce_scatter | solution.py:139
  96.8 125.9 %all-reduce.4.cloned.1.call-start = ((), (), s32[]{:S(2)}) async-start(), calls=%async_computation.6 | async-start | bytes 1179648 | tf_op jit(solution)/shard_map/psum | solution.py:166
  103.6 11.3 %copy-start.8 = (f32[128]{0:T(128)S(1)}, f32[128]{0:T(128)}, u32[]{:S(2)}) copy-start(f32[128]{0:T(128)} %param.18) | copy-start | bytes 1540
  117.9 11.7 %copy-start.1 = (bf16[32,32,256]{2,1,0:T(8,128)(2,1)S(1)}, bf16[32,32,256]{2,1,0:T(8,128)(2,1)}, u32[]{:S(2)}) copy-start(bf16[32,32,256]{2,1,0:T(8,128)(2,1)} %param.10) | copy-start | bytes 1572868
  117.9 11.7 %copy-start.4 = (f32[256]{0:T(256)S(1)}, f32[256]{0:T(256)}, u32[]{:S(2)}) copy-start(f32[256]{0:T(256)} %param.13) | copy-start | bytes 3076
  117.9 11.7 %copy-start.6 = (f32[256]{0:T(256)S(1)}, f32[256]{0:T(256)}, u32[]{:S(2)}) copy-start(f32[256]{0:T(256)} %param.14) | copy-start | bytes 3076
  117.9 12.9 %copy-start.5 = (bf16[256,64]{0,1:T(8,128)(2,1)S(1)}, bf16[256,64]{0,1:T(8,128)(2,1)}, u32[]{:S(2)}) copy-start(bf16[256,64]{0,1:T(8,128)(2,1)} %param.15) | copy-start | bytes 98308
Sparse Core Ops, SparseCore 0:
  32.2 18.4 all-gather.2
  82.6 20.7 reduce-scatter.2
  106.3 21.8 reduce-scatter.4
  132.1 90.4 all-reduce.3
where the time goes:
time: 234 us; the launch traced here: 233 us
  waiting for transfers between devices  68.6 us (29%)
  blocking collectives  64 us (27%)
  local copies, waits for them, and re-layouts  62.6 us (27%)
  matrix products  15.8 us (7%)
  between operations  14.7 us (6%)
  other arithmetic  6.5 us (3%)
    psum x1, waiting for transfers between devices, shards(): lax.psum((grad_out_w, weight_local, bias_local, gain_local, shift_local),...  59.4 us
    psum x1, blocking collectives, shards(): lax.psum((grad_out_w, weight_local, bias_local, gain_local, shift_local),...  30.2 us
    reshape x2, local copies, waits for them, and re-layouts, outer_adjoint(): return arranged.reshape(count_i * hidden, width_j * hidden)  22.7 us
    all_gather x1, blocking collectives, shards(): gathered = lax.all_gather(stacked, 'row', axis=0, tiled=True)  17.4 us
    all_to_all x1, blocking collectives, shards(): lax.all_to_all(left_tile, 'row', split_axis=0, concat_axis=1, tiled=True)  16.4 us
    convert_element_type x1, local copies, waits for them, and re-layouts, outer_block(): product.reshape(count_i * width_j, hidden * hidden).astype(jnp.bfloat16)  11.3 us
    transpose x1, local copies, waits for them, and re-layouts, outer_adjoint(): grad_outer.reshape(count_i, width_j, hidden, hidden).transpose(0, 2, 1, 3)  10.5 us
    reduce_scatter x1, waiting for transfers between devices, shards(): lax.psum_scatter(grad_right, 'row', scatter_dimension=0, tiled=True)  9.09 us
  transfers between devices with their start and end apart: 4, of which 2 were waited for; matrix products, arithmetic and copies ran while one was open for 30% of the time, Pallas kernels for 0%

commit v1 on v0

v1 whole, which is shorter than its diff:
```python
import functools

import jax
import jax.numpy as jnp
from jax import lax
from jax.experimental import pallas as pl
from jax.experimental.pallas import tpu as pltpu
from jax.sharding import PartitionSpec as P

EPSILON = 1e-05
LANES = 128
MESH = pl.DeviceIdType.MESH


def normalize(values, layer_norm_gain, norm_shift):
    widened = values.astype(jnp.float32)
    centred = widened - jnp.mean(widened, axis=-1, keepdims=True)
    inverse_deviation = lax.rsqrt(jnp.mean(centred * centred, axis=-1, keepdims=True) + EPSILON)
    scaled_product = centred * inverse_deviation
    return (
        scaled_product,
        inverse_deviation,
        (scaled_product * layer_norm_gain + norm_shift).astype(jnp.bfloat16),
    )


def layer_norm_backward_pass(
    normalized_input_gradient, scaled_product, inverse_deviation, layer_norm_gain
):
    grad_scaled = normalized_input_gradient * layer_norm_gain
    first = jnp.mean(grad_scaled, axis=-1, keepdims=True)
    second = jnp.mean(grad_scaled * scaled_product, axis=-1, keepdims=True)
    return inverse_deviation * (grad_scaled - first - scaled_product * second)


def route_gather_row(rows, cols):
    return dict(
        sends=rows,
        slots=rows,
        send=lambda t, r, c: (None, lax.rem(r + t, rows), c),
        mine=lambda r, c: r,
        source=lambda s, r, c: (s, c),
    )


def route_scatter_row(rows, cols):
    return dict(
        sends=rows,
        slots=rows,
        send=lambda t, r, c: (lax.rem(r + t, rows), lax.rem(r + t, rows), c),
        mine=lambda r, c: r,
        source=lambda s, r, c: (s, c),
    )


def route_tiles(rows, cols):
    factor = cols // rows
    return dict(
        sends=cols,
        slots=rows * factor,
        send=lambda t, r, c: (None, c // factor, lax.rem(c + t, cols)),
        mine=lambda r, c: r * factor + lax.rem(c, factor),
        source=lambda s, r, c: (s // factor, r * factor + lax.rem(s, factor)),
    )


def route_untile(rows, cols):
    factor = cols // rows

    def send(t, r, c):
        piece = lax.rem(r * factor + t, rows * factor)
        return piece, piece // factor, r * factor + lax.rem(piece, factor)

    return dict(
        sends=rows * factor,
        slots=cols,
        send=send,
        mine=lambda r, c: c,
        source=lambda s, r, c: (c // factor, s),
    )


def route_scatter_all(rows, cols):
    count = rows * cols

    def send(t, r, c):
        goal = lax.rem(r * cols + c + t, count)
        return goal, goal // cols, lax.rem(goal, cols)

    return dict(
        sends=count,
        slots=count,
        send=send,
        mine=lambda r, c: r * cols + c,
        source=lambda s, r, c: (s // cols, lax.rem(s, cols)),
    )


def route_gather_all(rows, cols):
    route = route_scatter_all(rows, cols)
    scatter_send = route["send"]
    route["send"] = lambda t, r, c: (None,) + scatter_send(t, r, c)[1:]
    return route


def exchange_kernel(routes, rows, cols, *refs):
    count = len(routes)
    sources, outs = refs[:count], refs[count : 2 * count]
    send_sems = refs[2 * count : 3 * count]
    recv_sems = refs[3 * count : 4 * count]
    local_sems = refs[4 * count]
    r = lax.axis_index("row")
    c = lax.axis_index("col")
    total = rows * cols
    barrier = pltpu.get_barrier_semaphore()

    def greet(t, carry):
        other = lax.rem(r * cols + c + t, total)
        pl.semaphore_signal(
            barrier,
            inc=1,
            device_id={"row": other // cols, "col": lax.rem(other, cols)},
            device_id_type=MESH,
        )
        return carry

    lax.fori_loop(1, total, greet, 0)
    pl.semaphore_wait(barrier, total - 1)

    def describe(k, t):
        piece, trow, tcol = routes[k]["send"](t, r, c)
        source = sources[k] if piece is None else sources[k].at[piece]
        slot = routes[k]["mine"](r, c)
        remote = pltpu.make_async_remote_copy(
            src_ref=source,
            dst_ref=outs[k].at[slot],
            send_sem=send_sems[k].at[t],
            recv_sem=recv_sems[k].at[slot],
            device_id={"row": trow, "col": tcol},
            device_id_type=MESH,
        )
        local = pltpu.make_async_copy(source, outs[k].at[slot], local_sems.at[k])
        here = jnp.logical_and(trow == r, tcol == c)
        return remote, local, here

    for k in range(count):

        def begin(t, carry, k=k):
            remote, local, here = describe(k, t)

            @pl.when(here)
            def _():
                local.start()
                local.wait()

            @pl.when(jnp.logical_not(here))
            def _():
                remote.start()

            return carry

        lax.fori_loop(0, routes[k]["sends"], begin, 0)

    for k in range(count):

        def finish(t, carry, k=k):
            remote, _, here = describe(k, t)

            @pl.when(jnp.logical_not(here))
            def _():
                remote.wait_send()

            return carry

        def receive(s, carry, k=k):
            srow, scol = routes[k]["source"](s, r, c)
            here = jnp.logical_and(srow == r, scol == c)
            arrival = pltpu.make_async_remote_copy(
                src_ref=outs[k].at[s],
                dst_ref=outs[k].at[s],
                send_sem=send_sems[k].at[0],
                recv_sem=recv_sems[k].at[s],
                device_id={"row": srow, "col": scol},
                device_id_type=MESH,
            )

            @pl.when(jnp.logical_not(here))
            def _():
                arrival.wait_recv()

            return carry

        lax.fori_loop(0, routes[k]["slots"], receive, 0)
        lax.fori_loop(0, routes[k]["sends"], finish, 0)


def exchange(arrays, makers, rows, cols, collective_id):
    routes = [maker(rows, cols) for maker in makers]
    shapes = []
    for array, route in zip(arrays, routes):
        block = array.shape if route["send"](0, 0, 0)[0] is None else array.shape[1:]
        shapes.append(jax.ShapeDtypeStruct((route["slots"],) + block, array.dtype))
    return pl.pallas_call(
        functools.partial(exchange_kernel, routes, rows, cols),
        out_shape=shapes,
        in_specs=[pl.BlockSpec(memory_space=pltpu.VMEM)] * len(arrays),
        out_specs=[pl.BlockSpec(memory_space=pltpu.VMEM)] * len(arrays),
        scratch_shapes=[pltpu.SemaphoreType.DMA((route["sends"],)) for route in routes]
        + [pltpu.SemaphoreType.DMA((route["slots"],)) for route in routes]
        + [pltpu.SemaphoreType.DMA((len(routes),))],
        compiler_params=pltpu.CompilerParams(collective_id=collective_id, has_side_effects=True),
    )(*arrays)


def pair_kernel(
    res,
    hidden,
    lt_ref,
    l_ref,
    r_ref,
    w_ref,
    cot_ref,
    div_ref,
    bias_ref,
    pair_ref,
    gw_ref,
    gl_ref,
    gr_ref,
    pre_ref,
    gpre_ref,
    glacc_ref,
):
    step = pl.program_id(0)
    fold = LANES // res
    seqs = r_ref.shape[0]
    major = l_ref.shape[0] // hidden

    @pl.when(step == 0)
    def _():
        gpre_ref[...] = (cot_ref[...].astype(jnp.float32) / div_ref[...]).astype(jnp.bfloat16)
        pre_ref[...] = jnp.zeros_like(pre_ref)
        glacc_ref[...] = jnp.zeros_like(glacc_ref)

    group = lax.broadcasted_iota(jnp.int32, (seqs, LANES), 1) // res
    wide = jnp.concatenate([group] * fold, axis=1)

    def spread(x):
        out = x
        for k in range(1, fold):
            out = out + pltpu.roll(x, k * res, 1)
        return out

    chunk = r_ref[...].astype(jnp.float32)
    copies = jnp.concatenate(
        [spread(jnp.where(group == d, chunk, 0.0)) for d in range(fold)], axis=1
    )
    masked = jnp.concatenate(
        [jnp.where(wide == i, copies, 0.0).astype(jnp.bfloat16) for i in range(fold)], axis=0
    )
    tile = jnp.dot(l_ref[...], masked, preferred_element_type=jnp.float32).astype(jnp.bfloat16)
    products = jnp.concatenate(
        [
            jnp.concatenate(
                [
                    tile[i * hidden : (i + 1) * hidden, d * LANES : (d + 1) * LANES]
                    for i in range(major)
                ],
                axis=1,
            )
            for d in range(fold)
        ],
        axis=0,
    )
    weight = w_ref[...]
    grad_pre = gpre_ref[...]
    pre_ref[...] += lax.dot_general(
        products, weight, (((0,), (0,)), ((), ())), preferred_element_type=jnp.float32
    )
    gw_ref[...] = jnp.dot(products, grad_pre, preferred_element_type=jnp.float32).astype(
        gw_ref.dtype
    )
    grad_products = lax.dot_general(
        weight, grad_pre, (((1,), (1,)), ((), ())), preferred_element_type=jnp.float32
    ).astype(jnp.bfloat16)
    grad_tile = jnp.concatenate(
        [
            jnp.concatenate(
                [
                    grad_products[d * hidden : (d + 1) * hidden, i * LANES : (i + 1) * LANES]
                    for d in range(fold)
                ],
                axis=1,
            )
            for i in range(major)
        ],
        axis=0,
    )
    glacc_ref[...] += lax.dot_general(
        masked, grad_tile, (((1,), (1,)), ((), ())), preferred_element_type=jnp.float32
    )
    grad_right = jnp.zeros((seqs, fold * LANES), jnp.float32)
    for i in range(fold):
        part = jnp.dot(
            lt_ref[i * seqs : (i + 1) * seqs, :], grad_tile, preferred_element_type=jnp.float32
        )
        grad_right = jnp.where(wide == i, part, grad_right)
    packed = jnp.zeros((seqs, LANES), jnp.float32)
    for d in range(fold):
        packed = jnp.where(
            group == d, spread(grad_right[:, d * LANES : (d + 1) * LANES]), packed
        )
    gr_ref[...] = packed.astype(gr_ref.dtype)

    @pl.when(step == pl.num_programs(0) - 1)
    def _():
        pair_ref[...] = ((pre_ref[...] + bias_ref[...]) / div_ref[...]).astype(pair_ref.dtype)
        gl_ref[...] = glacc_ref[...].astype(gl_ref.dtype)


def pair_tile(lt, right, weight, cotangent, divisor, bias, res, hidden):
    fold = LANES // res
    pairs, width = cotangent.shape
    seqs = right.shape[0]
    rows = lt.shape[1]

    def whole(shape):
        return pl.BlockSpec(shape, lambda k: (0,) * len(shape))

    return pl.pallas_call(
        functools.partial(pair_kernel, res, hidden),
        grid=(hidden // fold,),
        in_specs=[
            whole(lt.shape),
            whole(lt.shape[::-1]),
            pl.BlockSpec((seqs, LANES), lambda k: (0, k)),
            pl.BlockSpec((fold * hidden, width), lambda k: (k, 0)),
            whole((pairs, width)),
            whole((pairs, 1)),
            whole((1, width)),
        ],
        out_specs=[
            whole((pairs, width)),
            pl.BlockSpec((fold * hidden, width), lambda k: (k, 0)),
            whole(lt.shape),
            pl.BlockSpec((seqs, LANES), lambda k: (0, k)),
        ],
        out_shape=[
            jax.ShapeDtypeStruct((pairs, width), jnp.bfloat16),
            jax.ShapeDtypeStruct((hidden * hidden, width), jnp.bfloat16),
            jax.ShapeDtypeStruct(lt.shape, jnp.bfloat16),
            jax.ShapeDtypeStruct((seqs, hidden * res), jnp.bfloat16),
        ],
        scratch_shapes=[
            pltpu.VMEM((pairs, width), jnp.float32),
            pltpu.VMEM((pairs, width), jnp.bfloat16),
            pltpu.VMEM((fold * seqs, rows), jnp.float32),
        ],
        compiler_params=pltpu.CompilerParams(dimension_semantics=("arbitrary",)),
    )(lt, lt.T, right, weight, cotangent, divisor, bias)


def shards(
    alignment,
    sequence_mask,
    residue_mask,
    layer_norm_gain,
    norm_shift,
    proj_weight,
    proj_bias,
    out_weight,
    out_bias,
    cotangent,
):
    rows = lax.axis_size("row")
    cols = lax.axis_size("col")
    total = rows * cols
    factor = cols // rows
    row_index = lax.axis_index("row")
    col_index = lax.axis_index("col")
    seq_local, res_local, channels = alignment.shape
    seqs = seq_local * rows
    hidden = proj_weight.shape[1] // 2
    pair_width = out_weight.shape[1]
    tile_rows = res_local * factor
    fold = LANES // res_local
    inner = res_local // fold
    scaled_product, inverse_deviation, normed = normalize(alignment, layer_norm_gain, norm_shift)
    seq_here = lax.dynamic_slice_in_dim(sequence_mask, row_index * seq_local, seq_local)
    res_here = lax.dynamic_slice_in_dim(residue_mask, col_index * res_local, res_local)
    live = (seq_here[:, None] * res_here[None, :]).astype(jnp.float32)
    projected = jnp.dot(
        normed.reshape(-1, channels), proj_weight, preferred_element_type=jnp.float32
    )
    projected = projected.reshape(seq_local, res_local, 2 * hidden) + proj_bias
    masked = (projected * live[:, :, None]).astype(jnp.bfloat16)
    left_send = (
        masked[:, :, :hidden]
        .reshape(seq_local, inner, fold, hidden)
        .transpose(2, 0, 1, 3)
        .reshape(fold, seq_local, inner * hidden)
    )
    right_send = masked[:, :, hidden:].transpose(0, 2, 1).reshape(seq_local, hidden * res_local)
    lefts, rights = exchange(
        [left_send, right_send], [route_tiles, route_gather_row], rows, cols, 0
    )
    lt = (
        lefts.reshape(rows, factor, fold, seq_local, inner * hidden)
        .transpose(2, 0, 3, 1, 4)
        .reshape(fold * seqs, factor * inner * hidden)
    )
    right = rights.reshape(seqs, hidden * res_local)
    kept_count = jnp.sum(sequence_mask).astype(jnp.float32)
    tile_live = lax.dynamic_slice_in_dim(residue_mask, row_index * tile_rows, tile_rows).astype(
        jnp.float32
    )
    column_live = res_here.astype(jnp.float32)
    divisor = jnp.maximum(kept_count * tile_live[:, None] * column_live[None, :], 1.0).reshape(
        -1, 1
    )
    swapped = (
        out_weight.reshape(hidden, hidden, pair_width)
        .transpose(1, 0, 2)
        .reshape(hidden * hidden, pair_width)
    )
    pair, grad_w, grad_lt, grad_r = pair_tile(
        lt,
        right,
        swapped,
        cotangent.reshape(-1, pair_width),
        divisor,
        out_bias.reshape(1, -1),
        res_local,
        hidden,
    )
    pair_output_update = pair.reshape(tile_rows, res_local, pair_width)
    left_parts = (
        grad_lt.reshape(fold, rows, seq_local, factor, inner * hidden)
        .transpose(1, 3, 0, 2, 4)
        .reshape(rows * factor, fold, seq_local, inner * hidden)
    )
    got_left, got_right, got_w = exchange(
        [
            left_parts,
            grad_r.reshape(rows, seq_local, hidden * res_local),
            grad_w.reshape(total, -1, pair_width),
        ],
        [route_untile, route_scatter_row, route_scatter_all],
        rows,
        cols,
        1,
    )
    grad_left = (
        jnp.sum(got_left.astype(jnp.float32), axis=0)
        .reshape(fold, seq_local, inner, hidden)
        .transpose(1, 2, 0, 3)
        .reshape(seq_local, res_local, hidden)
    )
    grad_right = (
        jnp.sum(got_right.astype(jnp.float32), axis=0)
        .reshape(seq_local, hidden, res_local)
        .transpose(0, 2, 1)
    )
    grad_w_here = jnp.sum(got_w.astype(jnp.float32), axis=0).astype(jnp.bfloat16)
    grad_projected = jnp.concatenate([grad_left, grad_right], axis=-1) * live[:, :, None]
    grad_low = grad_projected.astype(jnp.bfloat16)
    normalized_input_gradient = jnp.dot(
        grad_low.reshape(-1, 2 * hidden), proj_weight.T, preferred_element_type=jnp.float32
    ).reshape(seq_local, res_local, channels)
    weight_local = lax.dot_general(
        normed.reshape(-1, channels),
        grad_low.reshape(-1, 2 * hidden),
        (((0,), (0,)), ((), ())),
        preferred_element_type=jnp.float32,
    )
    bias_local = jnp.sum(grad_projected, axis=(0, 1))
    gain_local = jnp.sum(normalized_input_gradient * scaled_product, axis=(0, 1))
    shift_local = jnp.sum(normalized_input_gradient, axis=(0, 1))
    alignment_gradient = layer_norm_backward_pass(
        normalized_input_gradient, scaled_product, inverse_deviation, layer_norm_gain
    ).astype(jnp.bfloat16)
    vectors = jnp.stack(
        [gain_local, shift_local, jnp.pad(bias_local, (0, channels - 2 * hidden))]
    )
    all_w, all_weight, all_vectors = exchange(
        [grad_w_here, weight_local.T.astype(jnp.bfloat16), vectors],
        [route_gather_all] * 3,
        rows,
        cols,
        2,
    )
    output_weight_gradient = (
        all_w.reshape(hidden, hidden, pair_width)
        .transpose(1, 0, 2)
        .reshape(hidden * hidden, pair_width)
        .astype(jnp.float32)
    )
    weight_sum = jnp.sum(all_weight.astype(jnp.float32), axis=0).T
    vector_sum = jnp.sum(all_vectors, axis=0)
    return (
        pair_output_update,
        alignment_gradient,
        vector_sum[0],
        vector_sum[1],
        weight_sum,
        vector_sum[2, : 2 * hidden],
        output_weight_gradient,
    )


def solution(mesh):
    return jax.shard_map(
        shards,
        mesh=mesh,
        in_specs=(
            P(("groups", "row"), "col", None),
            P("groups"),
            P("groups"),
            P(),
            P(),
            P(),
            P(),
            P(),
            P(),
            P(("groups", "row"), "col", None),
        ),
        out_specs=(
            P(("groups", "row"), "col", None),
            P(("groups", "row"), "col", None),
            P("groups"),
            P("groups"),
            P("groups", None),
            P("groups"),
            P("groups", None),
        ),
        check_vma=False,
    )
```

time: 234 us -> 118 us (0.50)
  Pallas kernels: 0 us -> 89.5 us
  waiting for transfers between devices: 68.6 us -> 0 us
  blocking collectives: 64 us -> 0 us
  local copies, waits for them, and re-layouts: 62.6 us -> 12.7 us
  matrix products: 15.8 us -> 2.37 us
  between operations: 14.7 us -> 1.51 us
  other arithmetic: 6.5 us -> 11.4 us
    pallas_call x0 -> x4, Pallas kernels: none -> 89.5 us  [the longest x3 74.9 us: exchange(): pl.pallas_call(functools.partial(exchange_kernel, routes, rows, cols), ou...]
    psum x1 -> x0, waiting for transfers between devices: 59.4 us -> none  [shards(): lax.psum((grad_out_w, weight_local, bias_local, gain_local, shift_local),...]
    psum x1 -> x0, blocking collectives: 30.2 us -> none  [shards(): lax.psum((grad_out_w, weight_local, bias_local, gain_local, shift_local),...]
    reshape x3 -> x9, local copies, waits for them, and re-layouts: 30.7 us -> 5.66 us  [the longest x1 1.67 us: shards(): grad_lt.reshape(fold, rows, seq_local, factor, inner * hidden)]
    all_gather x1 -> x0, blocking collectives: 17.4 us -> none  [shards(): gathered = lax.all_gather(stacked, 'row', axis=0, tiled=True)]
    all_to_all x1 -> x0, blocking collectives: 16.4 us -> none  [shards(): lax.all_to_all(left_tile, 'row', split_axis=0, concat_axis=1, tiled=True)]
    dot_general x6 -> x0, matrix products: 12.3 us -> none  [the longest x1 5.58 us: outer_block(): lax.dot_general(left_block, right_flat, (((0,), (0,)), ((), ())), preferr...]
    convert_element_type x1, local copies, waits for them, and re-layouts: 11.3 us -> 1.1 us  [shards(): output_weight_gradient = all_w.reshape(hidden, hidden, pair_width).transp...]
  transfers between devices with their start and end apart: 4 -> 0, of which waited for: 2 -> 0; matrix products, arithmetic and copies ran while one was open for 30% -> 0% of each run, Pallas kernels for 0% -> 0%
where the time goes in v1:
time: 118 us; the launch traced here: 117 us
  Pallas kernels  89.5 us (76%)
  local copies, waits for them, and re-layouts  12.7 us (11%)
  other arithmetic  11.4 us (10%)
  matrix products  2.37 us (2%)
  between operations  1.51 us (1%)
    pallas_call x3, Pallas kernels, exchange(): pl.pallas_call(functools.partial(exchange_kernel, routes, rows, cols), ou...  74.9 us
    pallas_call x1, Pallas kernels, pair_tile(): pl.pallas_call(functools.partial(pair_kernel, res, hidden), grid=(hidden...  14.6 us

profile of v1, /device:TPU:0, one launch (start us, length us, event | category | flops | bytes accessed | tf_op | source)
XLA Modules:
  0.0 117.5 jit_solution(18344350938371328469)
XLA Ops:
  0.7 1.4 %reduce_sum.122 = s32[]{:T(128)} reduce(s32[128]{0:T(128)} %param.11, s32[]{:T(128)} %constant.24.clone.1), dimensions={0}, to_apply=%region_2.0 | reduce | flops 127 | bytes 520 | tf_op jit(solution)/shard_map/reduce_sum | solution.py:412
  2.7 0.7 convert_multiply_fusion
  3.4 0.7 dynamic_slice.9
  4.1 0.7 fusion.25
  5.0 1.3 %convert_reduce_fusion = f32[32,32]{1,0:T(8,128)S(1)} fusion(bf16[32,32,256]{2,1,0:T(8,128)(2,1)} %param.10), kind=kLoop, calls=%fused_computation.1 | loop fusion | flops 523264 | bytes 528384 | tf_op jit(solution)/shard_map/reduce_sum | solution.py:17
  8.3 0.8 copy.27
  9.4 0.9 reshape.179.refs_1_
  10.4 0.8 reshape.178.refs_0_
  11.2 25.0 %shard_map.153 = (bf16[4,4,32,256]{3,2,1,0:T(8,128)(2,1)}, bf16[4,32,1024]{2,1,0:T(8,128)(2,1)}) custom-call(bf16[4,32,256]{2,1,0:T(8,128)(2,1)} %reshape.178.refs_0_, bf16[32,1024]{1,0:T(8,128)(2,1)} %reshape.179.refs_1_), custom_call_target="tpu_custom_call" | custom-call | tf_op jit(solution)/shard_map/pallas_call | solution.py:203
  36.2 1.0 copy.25
  37.2 0.9 copy.26
  38.1 1.3 %max.19.div_ref = f32[1024,1]{1,0:T(8,128)} reshape(f32[32,32]{1,0:T(8,128)S(1)} %multiply_maximum_fusion) | data formatting | bytes 8192 | tf_op jit(solution)/shard_map/max | solution.py:417
  39.4 14.6 %shard_map.154 = (bf16[1024,128]{1,0:T(8,128)(2,1)}, bf16[1024,128]{1,0:T(8,128)(2,1)}, bf16[512,256]{1,0:T(8,128)(2,1)}, bf16[128,1024]{1,0:T(8,128)(2,1)}) custom-call(bf16[512,256]{1,0:T(8,128)(2,1)} %bitcast.59, bf16[256,512]{1,0:T(8,128)(2,1)} %bitcast.66, bf16[128,1024]{1,0:T(8,128)(2,1)} %bitcast.76, bf16[1024,128]{1,0:T(8,128)(2,1)} %bitcast.65, ...), custom_call_target="tpu_custom_call" | custom-call | tf_op jit(solution)/shard_map/pallas_call | solution.py:329
  54.0 1.7 %copy.35 = bf16[4,4,32,1,256]{4,2,0,1,3:T(8,128)(2,1)} copy(bf16[4,4,32,1,256]{4,2,1,0,3:T(8,128)(2,1)} %bitcast.73) | data formatting | bytes 524288 | tf_op jit(solution)/shard_map/reshape | solution.py:437
  55.7 22.9 %shard_map.155 = (bf16[4,4,32,256]{3,2,1,0:T(8,128)(2,1)}, bf16[4,32,1024]{2,1,0:T(8,128)(2,1)}, bf16[16,64,128]{2,1,0:T(8,128)(2,1)}) custom-call(bf16[4,4,32,256]{3,2,1,0:T(8,128)(2,1)} %bitcast.63, bf16[4,32,1024]{2,1,0:T(8,128)(2,1)} %bitcast.71, bf16[16,64,128]{2,1,0:T(8,128)(2,1)} %bitcast.70), custom_call_target="tpu_custom_call" | custom-call | tf_op jit(solution)/shard_map/pallas_call | solution.py:203
  78.6 1.1 convert_reduce_fusion.3
  79.7 0.7 reduce_sum.127.refs_0_
  81.6 1.2 fusion.8.refs_1_
  82.8 0.7 fusion.15
  84.1 1.4 %fusion.14 = bf16[32,32,256]{2,1,0:T(8,128)(2,1)} fusion(bf16[32,32,256]{2,1,0:T(8,128)(2,1)S(1)} %copy-done.1, f32[32,32,256]{2,1,0:T(8,128)S(1)} %get-tuple-element.43, f32[32,32]{1,0:T(8,128)S(1)} %get-tuple-element.44, f32[32,32]{1,0:T(8,128)S(1)} %get-tuple-element.45, f32[256]{0:T(256)S(1)} %copy-done.7, f32[32,32]{1,0:T(8,128)S(1)} %add_rsqrt_fusion, ...), kind=kLoop, calls=%fused_computation.18 | loop fusion | flops 2359296 | bytes 2114560 | tf_op jit(solution)/shard_map/convert_element_type | solution.py:480
  85.5 27.0 %shard_map.156 = (bf16[16,64,128]{2,1,0:T(8,128)(2,1)}, bf16[16,64,256]{2,1,0:T(8,128)(2,1)}, f32[16,3,256]{2,1,0:T(4,128)}) custom-call(bf16[64,128]{1,0:T(8,128)(2,1)} %reduce_sum.127.refs_0_, bf16[64,256]{1,0:T(8,128)(2,1)} %fusion.8.refs_1_, f32[3,256]{1,0:T(4,128)} %pad_maximum_fusion.refs_2_), custom_call_target="tpu_custom_call" | custom-call | tf_op jit(solution)/shard_map/pallas_call | solution.py:203
  112.5 0.9 reduce_sum.131
  114.5 1.8 %convert_reduce_fusion.1 = f32[64,256]{1,0:T(8,128)} fusion(bf16[16,64,256]{2,1,0:T(8,128)(2,1)} %get-tuple-element.29), kind=kLoop, calls=%fused_computation.21 | loop fusion | flops 507904 | bytes 589824 | tf_op jit(solution)/shard_map/reduce_sum | solution.py:497
  116.4 1.1 copy.32
  (41 shorter events, 5.5 us)
Async XLA Ops:
  0.6 6.1 %copy-start = (bf16[256,64]{0,1:T(8,128)(2,1)S(1)}, bf16[256,64]{0,1:T(8,128)(2,1)}, u32[]{:S(2)}) copy-start(bf16[256,64]{0,1:T(8,128)(2,1)} %param.15) | copy-start | bytes 98308
  0.6 5.6 %copy-start.1 = (bf16[32,32,256]{2,1,0:T(8,128)(2,1)S(1)}, bf16[32,32,256]{2,1,0:T(8,128)(2,1)}, u32[]{:S(2)}) copy-start(bf16[32,32,256]{2,1,0:T(8,128)(2,1)} %param.10) | copy-start | bytes 1572868
  6.7 0.7 copy-start.7
  6.7 0.7 copy-start.8
  6.7 0.7 copy-start.9
  7.4 1.0 copy-start.5
  37.2 0.9 copy-start.2
  78.6 1.1 copy-start.6
  78.6 1.7 %copy-start.4 = (bf16[4,32,1024]{2,1,0:T(8,128)(2,1)S(1)}, bf16[4,32,1024]{2,1,0:T(8,128)(2,1)}, u32[]{:S(2)}) copy-start(bf16[4,32,1024]{2,1,0:T(8,128)(2,1)} %get-tuple-element.26) | copy-start | bytes 786436
  114.5 1.8 %copy-start.3 = (bf16[16,64,128]{2,1,0:T(8,128)(2,1)S(1)}, bf16[16,64,128]{2,1,0:T(8,128)(2,1)}, u32[]{:S(2)}) copy-start(bf16[16,64,128]{2,1,0:T(8,128)(2,1)} %get-tuple-element.30) | copy-start | bytes 786436

commit v2 on v1

--- a/solution.py
+++ b/solution.py
@@ -53,6 +53,26 @@
     )
 
 
+def route_gather_col(rows, cols):
+    return dict(
+        sends=cols,
+        slots=cols,
+        send=lambda t, r, c: (None, r, lax.rem(c + t, cols)),
+        mine=lambda r, c: c,
+        source=lambda s, r, c: (r, s),
+    )
+
+
+def route_scatter_col(rows, cols):
+    return dict(
+        sends=cols,
+        slots=cols,
+        send=lambda t, r, c: (lax.rem(c + t, cols), r, lax.rem(c + t, cols)),
+        mine=lambda r, c: c,
+        source=lambda s, r, c: (r, s),
+    )
+
+
 def route_tiles(rows, cols):
     factor = cols // rows
     return dict(
@@ -103,7 +123,7 @@
     return route
 
 
-def exchange_kernel(routes, rows, cols, *refs):
+def exchange_kernel(routes, rows, cols, along_row, *refs):
     count = len(routes)
     sources, outs = refs[:count], refs[count : 2 * count]
     send_sems = refs[2 * count : 3 * count]
@@ -111,15 +131,19 @@
     local_sems = refs[4 * count]
     r = lax.axis_index("row")
     c = lax.axis_index("col")
-    total = rows * cols
+    total = rows if along_row else rows * cols
     barrier = pltpu.get_barrier_semaphore()
 
     def greet(t, carry):
-        other = lax.rem(r * cols + c + t, total)
+        if along_row:
+            orow, ocol = lax.rem(r + t, total), c
+        else:
+            other = lax.rem(r * cols + c + t, total)
+            orow, ocol = other // cols, lax.rem(other, cols)
         pl.semaphore_signal(
             barrier,
             inc=1,
-            device_id={"row": other // cols, "col": lax.rem(other, cols)},
+            device_id={"row": orow, "col": ocol},
             device_id_type=MESH,
         )
         return carry
@@ -139,17 +163,17 @@
             device_id={"row": trow, "col": tcol},
             device_id_type=MESH,
         )
-        local = pltpu.make_async_copy(source, outs[k].at[slot], local_sems.at[k])
         here = jnp.logical_and(trow == r, tcol == c)
-        return remote, local, here
+        return remote, source, outs[k].at[slot], here
 
     for k in range(count):
 
         def begin(t, carry, k=k):
-            remote, local, here = describe(k, t)
+            remote, source, target, here = describe(k, t)
 
             @pl.when(here)
             def _():
+                local = pltpu.make_async_copy(source, target, local_sems.at[k])
                 local.start()
                 local.wait()
 
@@ -164,7 +188,7 @@
     for k in range(count):
 
         def finish(t, carry, k=k):
-            remote, _, here = describe(k, t)
+            remote, _, _, here = describe(k, t)
 
             @pl.when(jnp.logical_not(here))
             def _():
@@ -194,14 +218,14 @@
         lax.fori_loop(0, routes[k]["sends"], finish, 0)
 
 
-def exchange(arrays, makers, rows, cols, collective_id):
+def exchange(arrays, makers, rows, cols, collective_id, along_row=False):
     routes = [maker(rows, cols) for maker in makers]
     shapes = []
     for array, route in zip(arrays, routes):
         block = array.shape if route["send"](0, 0, 0)[0] is None else array.shape[1:]
         shapes.append(jax.ShapeDtypeStruct((route["slots"],) + block, array.dtype))
     return pl.pallas_call(
-        functools.partial(exchange_kernel, routes, rows, cols),
+        functools.partial(exchange_kernel, routes, rows, cols, along_row),
         out_shape=shapes,
         in_specs=[pl.BlockSpec(memory_space=pltpu.VMEM)] * len(arrays),
         out_specs=[pl.BlockSpec(memory_space=pltpu.VMEM)] * len(arrays),
@@ -373,7 +397,6 @@
 ):
     rows = lax.axis_size("row")
     cols = lax.axis_size("col")
-    total = rows * cols
     factor = cols // rows
     row_index = lax.axis_index("row")
     col_index = lax.axis_index("col")
@@ -442,9 +465,9 @@
         [
             left_parts,
             grad_r.reshape(rows, seq_local, hidden * res_local),
-            grad_w.reshape(total, -1, pair_width),
-        ],
-        [route_untile, route_scatter_row, route_scatter_all],
+            grad_w.reshape(cols, -1, pair_width),
+        ],
+        [route_untile, route_scatter_row, route_scatter_col],
         rows,
         cols,
         1,
@@ -460,7 +483,7 @@
         .reshape(seq_local, hidden, res_local)
         .transpose(0, 2, 1)
     )
-    grad_w_here = jnp.sum(got_w.astype(jnp.float32), axis=0).astype(jnp.bfloat16)
+    grad_w_col = jnp.sum(got_w.astype(jnp.float32), axis=0).astype(jnp.bfloat16)
     grad_projected = jnp.concatenate([grad_left, grad_right], axis=-1) * live[:, :, None]
     grad_low = grad_projected.astype(jnp.bfloat16)
     normalized_input_gradient = jnp.dot(
@@ -481,15 +504,33 @@
     vectors = jnp.stack(
         [gain_local, shift_local, jnp.pad(bias_local, (0, channels - 2 * hidden))]
     )
-    all_w, all_weight, all_vectors = exchange(
-        [grad_w_here, weight_local.T.astype(jnp.bfloat16), vectors],
-        [route_gather_all] * 3,
+    row_w, row_weight, row_vectors = exchange(
+        [
+            grad_w_col.reshape(rows, -1, pair_width),
+            weight_local.T.astype(jnp.bfloat16),
+            vectors,
+        ],
+        [route_scatter_row, route_gather_row, route_gather_row],
         rows,
         cols,
         2,
+        along_row=True,
+    )
+    all_w, all_weight, all_vectors = exchange(
+        [
+            jnp.sum(row_w.astype(jnp.float32), axis=0).astype(jnp.bfloat16),
+            jnp.sum(row_weight.astype(jnp.float32), axis=0).astype(jnp.bfloat16),
+            jnp.sum(row_vectors, axis=0),
+        ],
+        [route_gather_all, route_gather_col, route_gather_col],
+        rows,
+        cols,
+        3,
     )
     output_weight_gradient = (
-        all_w.reshape(hidden, hidden, pair_width)
+        all_w.reshape(rows, cols, -1, pair_width)
+        .transpose(1, 0, 2, 3)
+        .reshape(hidden, hidden, pair_width)
         .transpose(1, 0, 2)
         .reshape(hidden * hidden, pair_width)
         .astype(jnp.float32)

time: 118 us -> 112 us (0.949)
  Pallas kernels: 89.5 us -> 78.9 us
  other arithmetic: 11.4 us -> 14.6 us
  local copies, waits for them, and re-layouts: 12.7 us -> 14 us
    pallas_call x3 -> x4, Pallas kernels: 74.9 us -> 64.3 us  [exchange(): pl.pallas_call(functools.partial(exchange_kernel, routes, rows, cols, alo...]
    reduce_sum x1 -> x4, other arithmetic: 0.65 us -> 4.29 us  [the longest x1 1.56 us: shards(): jnp.sum(row_weight.astype(jnp.float32), axis=0).astype(jnp.bfloat16)]
where the time goes in v2:
time: 112 us; the launch traced here: 111 us
  Pallas kernels  78.9 us (70%)
  other arithmetic  14.6 us (13%)
  local copies, waits for them, and re-layouts  14 us (12%)
  matrix products  2.37 us (2%)
  between operations  1.52 us (1%)
    pallas_call x4, Pallas kernels, exchange(): pl.pallas_call(functools.partial(exchange_kernel, routes, rows, cols, alo...  64.3 us
    pallas_call x1, Pallas kernels, pair_tile(): pl.pallas_call(functools.partial(pair_kernel, res, hidden), grid=(hidden...  14.6 us

profile of v2, /device:TPU:0, one launch (start us, length us, event | category | flops | bytes accessed | tf_op | source)
XLA Modules:
  0.0 111.3 jit_solution(5561963414773482310)
XLA Ops:
  0.7 1.4 %reduce_sum.155 = s32[]{:T(128)} reduce(s32[128]{0:T(128)} %param.11, s32[]{:T(128)} %constant.26.clone.1), dimensions={0}, to_apply=%region_2.0 | reduce | flops 127 | bytes 520 | tf_op jit(solution)/shard_map/reduce_sum | solution.py:435
  2.7 0.7 convert_multiply_fusion
  5.0 1.3 %convert_reduce_fusion = f32[32,32]{1,0:T(8,128)S(1)} fusion(bf16[32,32,256]{2,1,0:T(8,128)(2,1)} %param.10), kind=kLoop, calls=%fused_computation.1 | loop fusion | flops 523264 | bytes 528384 | tf_op jit(solution)/shard_map/reduce_sum | solution.py:17
  8.3 0.8 copy.36
  9.4 0.9 reshape.185.refs_1_
  10.4 0.8 reshape.184.refs_0_
  11.2 25.0 %shard_map.153 = (bf16[4,4,32,256]{3,2,1,0:T(8,128)(2,1)}, bf16[4,32,1024]{2,1,0:T(8,128)(2,1)}) custom-call(bf16[4,32,256]{2,1,0:T(8,128)(2,1)} %reshape.184.refs_0_, bf16[32,1024]{1,0:T(8,128)(2,1)} %reshape.185.refs_1_), custom_call_target="tpu_custom_call" | custom-call | tf_op jit(solution)/shard_map/pallas_call | solution.py:227
  36.2 1.0 copy.34
  37.2 0.9 copy.35
  38.1 1.3 %max.19.div_ref = f32[1024,1]{1,0:T(8,128)} reshape(f32[32,32]{1,0:T(8,128)S(1)} %multiply_maximum_fusion) | data formatting | bytes 8192 | tf_op jit(solution)/shard_map/max | solution.py:440
  39.4 14.6 %shard_map.154 = (bf16[1024,128]{1,0:T(8,128)(2,1)}, bf16[1024,128]{1,0:T(8,128)(2,1)}, bf16[512,256]{1,0:T(8,128)(2,1)}, bf16[128,1024]{1,0:T(8,128)(2,1)}) custom-call(bf16[512,256]{1,0:T(8,128)(2,1)} %bitcast.63, bf16[256,512]{1,0:T(8,128)(2,1)} %bitcast.71, bf16[128,1024]{1,0:T(8,128)(2,1)} %bitcast.82, bf16[1024,128]{1,0:T(8,128)(2,1)} %bitcast.70, ...), custom_call_target="tpu_custom_call" | custom-call | tf_op jit(solution)/shard_map/pallas_call | solution.py:353
  54.0 1.7 %copy.45 = bf16[4,4,32,1,256]{4,2,0,1,3:T(8,128)(2,1)} copy(bf16[4,4,32,1,256]{4,2,1,0,3:T(8,128)(2,1)} %bitcast.79) | data formatting | bytes 524288 | tf_op jit(solution)/shard_map/reshape | solution.py:460
  55.7 17.4 %shard_map.155 = (bf16[4,4,32,256]{3,2,1,0:T(8,128)(2,1)}, bf16[4,32,1024]{2,1,0:T(8,128)(2,1)}, bf16[4,256,128]{2,1,0:T(8,128)(2,1)}) custom-call(bf16[4,4,32,256]{3,2,1,0:T(8,128)(2,1)} %bitcast.68, bf16[4,32,1024]{2,1,0:T(8,128)(2,1)} %bitcast.76, bf16[4,256,128]{2,1,0:T(8,128)(2,1)} %bitcast.75), custom_call_target="tpu_custom_call" | custom-call | tf_op jit(solution)/shard_map/pallas_call | solution.py:227
  73.1 1.0 convert_reduce_fusion.2
  76.4 1.2 %fusion.8.refs_1_ = bf16[64,256]{1,0:T(8,128)(2,1)} fusion(bf16[32,32,256]{2,1,0:T(8,128)(2,1)S(1)} %copy-done.1, f32[256]{0:T(256)S(1)} %copy-done.8, f32[256]{0:T(256)S(1)} %copy-done.7, f32[32,32]{1,0:T(8,128)S(1)} %add_rsqrt_fusion, f32[32,32]{1,0:T(8,128)S(1)} %broadcast_multiply_fusion.2, bf16[32,32,64]{2,1,0:T(8,128)(2,1)S(1)} %get-tuple-element.42), kind=kOutput, calls=%fused_computation.12 | convolution fusion | flops 35143680 | bytes 698368 | tf_op jit(solution)/shard_map/dot_general | solution.py:492
  77.6 0.7 fusion.15
  78.9 1.4 %fusion.14 = bf16[32,32,256]{2,1,0:T(8,128)(2,1)} fusion(bf16[32,32,256]{2,1,0:T(8,128)(2,1)S(1)} %copy-done.1, f32[32,32,256]{2,1,0:T(8,128)S(1)} %get-tuple-element.49, f32[32,32]{1,0:T(8,128)S(1)} %get-tuple-element.50, f32[32,32]{1,0:T(8,128)S(1)} %get-tuple-element.51, f32[256]{0:T(256)S(1)} %copy-done.7, f32[32,32]{1,0:T(8,128)S(1)} %add_rsqrt_fusion, ...), kind=kLoop, calls=%fused_computation.18 | loop fusion | flops 2359296 | bytes 2114560 | tf_op jit(solution)/shard_map/convert_element_type | solution.py:503
  80.3 10.7 %shard_map.156 = (bf16[4,64,128]{2,1,0:T(8,128)(2,1)}, bf16[4,64,256]{2,1,0:T(8,128)(2,1)}, f32[4,3,256]{2,1,0:T(4,128)}) custom-call(bf16[4,64,128]{2,1,0:T(8,128)(2,1)} %bitcast.77, bf16[64,256]{1,0:T(8,128)(2,1)} %fusion.8.refs_1_, f32[3,256]{1,0:T(4,128)} %pad_maximum_fusion.refs_2_), custom_call_target="tpu_custom_call" | custom-call | tf_op jit(solution)/shard_map/pallas_call | solution.py:227
  91.1 1.5 %reduce_sum.164.refs_0_ = bf16[64,128]{1,0:T(8,128)(2,1)} reduce(bf16[4,64,128]{2,1,0:T(8,128)(2,1)} %get-tuple-element.31, bf16[]{:T(256)} %constant.29.clone.1), dimensions={0}, to_apply=%region_11.12 | reduce | flops 24576 | bytes 81922 | tf_op jit(solution)/shard_map/reduce_sum | solution.py:521
  92.5 1.6 %reduce_sum.165.refs_1_ = bf16[64,256]{1,0:T(8,128)(2,1)} reduce(bf16[4,64,256]{2,1,0:T(8,128)(2,1)} %get-tuple-element.32, bf16[]{:T(256)} %constant.29.clone.1), dimensions={0}, to_apply=%region_12.13 | reduce | flops 49152 | bytes 163842 | tf_op jit(solution)/shard_map/reduce_sum | solution.py:522
  94.7 11.1 %shard_map.157 = (bf16[16,64,128]{2,1,0:T(8,128)(2,1)}, bf16[4,64,256]{2,1,0:T(8,128)(2,1)}, f32[4,3,256]{2,1,0:T(4,128)}) custom-call(bf16[64,128]{1,0:T(8,128)(2,1)} %reduce_sum.164.refs_0_, bf16[64,256]{1,0:T(8,128)(2,1)} %reduce_sum.165.refs_1_, f32[3,256]{1,0:T(4,128)} %reduce_sum.166.refs_2_), custom_call_target="tpu_custom_call" | custom-call | tf_op jit(solution)/shard_map/pallas_call | solution.py:227
  107.7 1.6 %convert_reduce_fusion.3 = f32[64,256]{1,0:T(8,128)} fusion(bf16[4,64,256]{2,1,0:T(8,128)(2,1)} %get-tuple-element.35), kind=kLoop, calls=%fused_computation.28 | loop fusion | flops 114688 | bytes 196608 | tf_op jit(solution)/shard_map/reduce_sum | solution.py:538
  109.2 1.0 copy.41
  110.2 1.1 copy.42
  (45 shorter events, 9.2 us)
Async XLA Ops:
  0.6 6.1 %copy-start = (bf16[256,64]{0,1:T(8,128)(2,1)S(1)}, bf16[256,64]{0,1:T(8,128)(2,1)}, u32[]{:S(2)}) copy-start(bf16[256,64]{0,1:T(8,128)(2,1)} %param.15) | copy-start | bytes 98308
  0.6 5.6 %copy-start.1 = (bf16[32,32,256]{2,1,0:T(8,128)(2,1)S(1)}, bf16[32,32,256]{2,1,0:T(8,128)(2,1)}, u32[]{:S(2)}) copy-start(bf16[32,32,256]{2,1,0:T(8,128)(2,1)} %param.10) | copy-start | bytes 1572868
  6.7 0.7 copy-start.7
  6.7 0.7 copy-start.8
  6.7 0.7 copy-start.9
  7.4 1.0 copy-start.5
  37.2 0.9 copy-start.2
  73.1 1.1 copy-start.3
  74.1 1.0 copy-start.4
  92.5 1.6 %copy-start.6 = (f32[4,3,256]{2,1,0:T(4,128)S(1)}, f32[4,3,256]{2,1,0:T(4,128)}, u32[]{:S(2)}) copy-start(f32[4,3,256]{2,1,0:T(4,128)} %get-tuple-element.33) | copy-start | bytes 36868
